TPU v7x, 32 devices: a whole 2x2x4 slice. The times are simulated.
32 devices in a mesh: dp: 4 (over y, x), rows: 8 (over z, core).
Axes of the slice: x: 2, y: 2, z: 4, core: 2. Of those that a mesh axis runs over, the one named last changes fastest.
Arguments:
- grad_out: bfloat16 [2048, 4096], P('dp', 'rows'), may hold values from -0.375 to 0.375
- activations: bfloat16 [2048, 4096], P('dp', 'rows'), may hold values from -6 to 6
- error_feedback: float32 [4, 4096, 4096], P('dp', 'rows'), may hold values from -6 to 6
- momentum: bfloat16 [4096, 4096], P('rows'), may hold values from -1.1953125 to 1.1953125
- right_factor: float32 [4096, 128], P('rows'), may hold values from -0.09375 to 0.09375
Outputs:
- new_error: float32 [4, 4096, 4096], P('dp', 'rows')
- new_momentum: bfloat16 [4096, 4096], P('rows')
- new_right: float32 [4096, 128], P('rows')
All inputs are finite; a program needn't handle non-finite values.
Results may differ from a plain program's by a relative error of at most 0.0012.
Values may be sent and summed in bfloat16 or wider, within the bound.
No kernel may reach another device: no remote copies, remote signals or barrier semaphores. Data moves between devices by JAX's collectives and lax.ppermute only.
A program may use at most 64 MiB of HBM per device.

v0:
```python
import jax
import jax.numpy as jnp
from jax import lax
from jax.sharding import PartitionSpec as P

PASSES = 2


MOMENTUM_RATE = 0.9
HIGHEST = lax.Precision.HIGHEST


def per_device(grad_out, activations, error_feedback, momentum, right_factor):
    replicas = lax.axis_size("dp")
    grad_local = lax.dot_general(
        grad_out,
        lax.all_gather(activations, "rows", axis=1, tiled=True),
        (((0,), (0,)), ((), ())),
        preferred_element_type=jnp.float32,
    )
    merged = grad_local + error_feedback[0]
    right_full = lax.all_gather(right_factor, "rows", axis=0, tiled=True)
    left_factor = None
    own_rows = None
    for pass_index in range(PASSES):
        local_term = jnp.dot(
            merged, right_full, precision=HIGHEST, preferred_element_type=jnp.float32
        )
        left_factor = lax.psum(local_term, "dp") / replicas
        gram_local = jnp.dot(
            left_factor.T, left_factor, precision=HIGHEST, preferred_element_type=jnp.float32
        )
        gram_matrix = lax.psum(gram_local, "rows")
        cholesky_lower = jnp.linalg.cholesky(gram_matrix)
        left_factor = jax.scipy.linalg.solve_triangular(cholesky_lower, left_factor.T, lower=True).T
        right_term = lax.dot_general(
            merged,
            left_factor,
            (((0,), (0,)), ((), ())),
            precision=HIGHEST,
            preferred_element_type=jnp.float32,
        )
        own_rows = lax.psum_scatter(right_term, "rows", scatter_dimension=0, tiled=True)
        own_rows = lax.psum(own_rows, "dp") / replicas
        right_full = lax.all_gather(own_rows, "rows", axis=0, tiled=True)
    approx = jnp.dot(
        left_factor, right_full.T, precision=HIGHEST, preferred_element_type=jnp.float32
    )
    new_error = (merged - approx)[None]
    new_momentum = (MOMENTUM_RATE * momentum.astype(jnp.float32) + approx).astype(jnp.bfloat16)
    return (new_error, new_momentum, own_rows)


def solution(mesh):
    return jax.shard_map(
        per_device,
        mesh=mesh,
        in_specs=(
            P("dp", "rows"),
            P("dp", "rows"),
            P("dp", "rows", None),
            P("rows", None),
            P("rows", None),
        ),
        out_specs=(P("dp", "rows", None), P("rows", None), P("rows", None)),
        check_vma=False,
    )
```

profile of v0, /device:TPU:0, one launch (start us, length us, event | category | flops | bytes accessed | tf_op | source)
XLA Modules:
  0.0 638.8 jit_solution(15261012926276648020)
XLA Ops:
  7.2 0.0 copy-start
  7.2 0.0 all-gather.5.cloned.1.call-start
  7.2 0.7 all-gather.5.cloned.1.call-update
  7.9 0.0 all-gather.7.cloned.1.call-start
  8.0 0.7 all-gather.7.cloned.1.call-update
  8.7 0.0 all-reduce.7.cloned.1.call-start
  8.7 50.5 %all-gather.5.cloned.1.call-done = bf16[512,4096]{1,0:T(8,128)(2,1)} async-done(((bf16[512,512]{1,0:T(8,128)(2,1)}), bf16[512,4096]{1,0:T(8,128)(2,1)}) %all-gather.5.cloned.1.call-update) | async-done | bytes 4194320 | tf_op jit(solution)/shard_map/all_gather | solution.py:17
  59.2 0.0 copy-done
  59.2 10.5 %bitcast_add_fusion = f32[512,4096]{1,0:T(8,128)} fusion(f32[1,512,4096]{2,1,0:T(8,128)} %param.10, bf16[512,512]{1,0:T(8,128)(2,1)S(1)} %copy-done, bf16[512,4096]{1,0:T(8,128)(2,1)} %all-gather.5.cloned.1.call-done), kind=kOutput, calls=%fused_computation | convolution fusion | flops 2149580800 | bytes 21495808 | tf_op jit(solution)/shard_map/dot_general | solution.py:15
  69.7 19.1 %all-gather.7.cloned.1.call-done = f32[4096,128]{1,0:T(8,128)} async-done(((f32[512,128]{1,0:T(8,128)}), f32[4096,128]{1,0:T(8,128)}) %all-gather.7.cloned.1.call-update) | async-done | bytes 2097168 | tf_op jit(solution)/shard_map/all_gather | solution.py:22
  88.8 10.0 %fusion.26 = f32[512,128]{1,0:T(8,128)} fusion(f32[512,4096]{1,0:T(8,128)} %bitcast_add_fusion, f32[4096,128]{1,0:T(8,128)} %all-gather.7.cloned.1.call-done), kind=kOutput, calls=%fused_computation.40 | convolution fusion | flops 3221225472 | bytes 10747904 | tf_op jit(solution)/shard_map/dot_general | solution.py:26
  98.8 0.0 all-reduce.7.cloned.1.call-update
  98.9 0.0 all-reduce.9.cloned.1.call-start
  98.9 42.5 %all-reduce.7.cloned.1.call-done = f32[512,128]{1,0:T(8,128)} async-done(((f32[512,128]{1,0:T(8,128)}), f32[512,128]{1,0:T(8,128)}) %all-reduce.7.cloned.1.call-update) | async-done | bytes 262160 | tf_op jit(solution)/shard_map/psum | solution.py:29
  141.5 2.3 fusion.8
  143.7 0.0 all-reduce.9.cloned.1.call-update
  143.7 0.3 reduce-scatter.3.cloned.1.call-start
  144.1 54.8 %all-reduce.9.cloned.1.call-done = f32[128,128]{0,1:T(8,128)} async-done(((f32[128,128]{0,1:T(8,128)}), f32[128,128]{0,1:T(8,128)}) %all-reduce.9.cloned.1.call-update) | async-done | bytes 65552 | tf_op jit(solution)/shard_map/psum | solution.py:33
  198.9 0.9 copy.9
  199.9 0.9 fusion.19
  200.7 11.7 %cholesky.44 = f32[128,128]{1,0:T(8,128)S(1)} custom-call(f32[128,128]{1,0:T(8,128)S(1)} %fusion.19), custom_call_target="Cholesky" | custom-call | tf_op jit(solution)/shard_map/jit(cholesky)/cholesky | solution.py:34
  212.5 0.6 compare_reduce_fusion.1
  213.1 0.7 fusion.14
  213.8 9.8 %custom-call.6 = f32[1,128,128]{1,2,0:T(8,128)S(1)} custom-call(f32[1,128,128]{2,1,0:T(8,128)S(1)} %fusion.14), custom_call_target="InvertDiagBlocksLowerTriangular" | custom-call | tf_op jit(solution)/shard_map/jit(_solve_triangular)/triangular_solve | solution.py:35
  223.6 1.4 fusion.2
  225.0 17.1 %fusion.27 = f32[4096,128]{1,0:T(8,128)} fusion(f32[512,4096]{1,0:T(8,128)} %bitcast_add_fusion, f32[128,512]{1,0:T(8,128)S(1)} %fusion.2), kind=kOutput, calls=%fused_computation.41 | convolution fusion | flops 3221225472 | bytes 10747904 | tf_op jit(solution)/shard_map/dot_general | solution.py:36
  242.0 0.0 reduce-scatter.3.cloned.1.call-update
  242.1 0.0 all-reduce.11.cloned.1.call-start
  242.1 35.2 %reduce-scatter.3.cloned.1.call-done = f32[512,128]{1,0:T(8,128)} async-done(((f32[4096,128]{1,0:T(8,128)}), f32[512,128]{1,0:T(8,128)}) %reduce-scatter.3.cloned.1.call-update) | async-done | bytes 262160 | tf_op jit(solution)/shard_map/reduce_scatter | solution.py:43
  277.3 0.0 all-reduce.11.cloned.1.call-update
  277.3 0.0 all-gather.9.cloned.1.call-start
  277.4 44.3 %all-reduce.11.cloned.1.call-done = f32[512,128]{1,0:T(8,128)} async-done(((f32[512,128]{1,0:T(8,128)}), f32[512,128]{1,0:T(8,128)}) %all-reduce.11.cloned.1.call-update) | async-done | bytes 262160 | tf_op jit(solution)/shard_map/psum | solution.py:44
  321.7 1.7 broadcast_multiply_fusion.1
  323.4 0.0 all-gather.9.cloned.1.call-update
  323.4 0.0 all-reduce.13.cloned.1.call-start
  323.5 29.6 %all-gather.9.cloned.1.call-done = f32[4096,128]{1,0:T(8,128)} async-done(((f32[512,128]{1,0:T(8,128)}), f32[4096,128]{1,0:T(8,128)}) %all-gather.9.cloned.1.call-update) | async-done | bytes 2097168 | tf_op jit(solution)/shard_map/all_gather | solution.py:45
  353.1 10.0 %fusion.28 = f32[512,128]{1,0:T(8,128)} fusion(f32[512,4096]{1,0:T(8,128)} %bitcast_add_fusion, f32[4096,128]{1,0:T(8,128)} %all-gather.9.cloned.1.call-done), kind=kOutput, calls=%fused_computation.42 | convolution fusion | flops 3221225472 | bytes 10747904 | tf_op jit(solution)/shard_map/dot_general | solution.py:26
  363.1 0.0 all-reduce.13.cloned.1.call-update
  363.2 0.0 all-reduce.15.cloned.1.call-start
  363.2 42.5 %all-reduce.13.cloned.1.call-done = f32[512,128]{1,0:T(8,128)} async-done(((f32[512,128]{1,0:T(8,128)}), f32[512,128]{1,0:T(8,128)}) %all-reduce.13.cloned.1.call-update) | async-done | bytes 262160 | tf_op jit(solution)/shard_map/psum | solution.py:29
  405.7 2.3 fusion.5
  408.0 0.0 all-reduce.15.cloned.1.call-update
  408.0 0.2 reduce-scatter.5.cloned.1.call-start
  408.3 55.1 %all-reduce.15.cloned.1.call-done = f32[128,128]{0,1:T(8,128)} async-done(((f32[128,128]{0,1:T(8,128)}), f32[128,128]{0,1:T(8,128)}) %all-reduce.15.cloned.1.call-update) | async-done | bytes 65552 | tf_op jit(solution)/shard_map/psum | solution.py:33
  463.4 0.9 copy.11
  464.3 0.9 fusion.17
  465.2 11.7 %cholesky.55 = f32[128,128]{1,0:T(8,128)S(1)} custom-call(f32[128,128]{1,0:T(8,128)S(1)} %fusion.17), custom_call_target="Cholesky" | custom-call | tf_op jit(solution)/shard_map/jit(cholesky)/cholesky | solution.py:34
  476.9 0.6 compare_reduce_fusion
  477.5 0.7 fusion.15
  478.2 9.8 %custom-call.7 = f32[1,128,128]{1,2,0:T(8,128)S(1)} custom-call(f32[1,128,128]{2,1,0:T(8,128)S(1)} %fusion.15), custom_call_target="InvertDiagBlocksLowerTriangular" | custom-call | tf_op jit(solution)/shard_map/jit(_solve_triangular)/triangular_solve | solution.py:35
  488.0 1.4 fusion
  489.4 16.8 %fusion.29 = f32[4096,128]{1,0:T(8,128)} fusion(f32[512,4096]{1,0:T(8,128)} %bitcast_add_fusion, f32[128,512]{1,0:T(8,128)S(1)} %fusion), kind=kOutput, calls=%fused_computation.43 | convolution fusion | flops 3221225472 | bytes 10747904 | tf_op jit(solution)/shard_map/dot_general | solution.py:36
  506.2 0.0 reduce-scatter.5.cloned.1.call-update
  506.2 0.0 all-reduce.17.cloned.1.call-start
  506.2 35.2 %reduce-scatter.5.cloned.1.call-done = f32[512,128]{1,0:T(8,128)} async-done(((f32[4096,128]{1,0:T(8,128)}), f32[512,128]{1,0:T(8,128)}) %reduce-scatter.5.cloned.1.call-update) | async-done | bytes 262160 | tf_op jit(solution)/shard_map/reduce_scatter | solution.py:43
  541.5 0.0 all-reduce.17.cloned.1.call-update
  541.5 0.0 all-gather.11.cloned.1.call-start
  541.5 44.5 %all-reduce.17.cloned.1.call-done = f32[512,128]{1,0:T(8,128)} async-done(((f32[512,128]{1,0:T(8,128)}), f32[512,128]{1,0:T(8,128)}) %all-reduce.17.cloned.1.call-update) | async-done | bytes 262160 | tf_op jit(solution)/shard_map/psum | solution.py:44
  586.1 1.7 broadcast_multiply_fusion
  587.7 0.0 all-gather.11.cloned.1.call-update
  587.8 29.5 %all-gather.11.cloned.1.call-done = f32[4096,128]{1,0:T(8,128)} async-done(((f32[512,128]{1,0:T(8,128)}), f32[4096,128]{1,0:T(8,128)}) %all-gather.11.cloned.1.call-update) | async-done | bytes 2097168 | tf_op jit(solution)/shard_map/all_gather | solution.py:45
  617.3 14.5 %add_convert_fusion = (bf16[512,4096]{1,0:T(8,128)(2,1)}, f32[1,512,4096]{2,1,0:T(8,128)}) fusion(bf16[512,4096]{1,0:T(8,128)(2,1)} %param.11, f32[512,4096]{1,0:T(8,128)} %bitcast_add_fusion, f32[128,512]{1,0:T(8,128)S(1)} %fusion, f32[4096,128]{1,0:T(8,128)} %all-gather.11.cloned.1.call-done), kind=kOutput, calls=%fused_computation.1 | convolution fusion | flops 3231711232 | bytes 27525120 | tf_op jit(solution)/shard_map/dot_general | solution.py:46
  (2 shorter events, 0.1 us)
Async XLA Ops:
  7.2 52.1 %copy-start = (bf16[512,512]{1,0:T(8,128)(2,1)S(1)}, bf16[512,512]{1,0:T(8,128)(2,1)}, u32[]{:S(2)}) copy-start(bf16[512,512]{1,0:T(8,128)(2,1)} %param.8) | copy-start | bytes 1572868
  7.2 52.0 %all-gather.5.cloned.1.call-start = ((), (), s32[]{:S(2)}) async-start(), calls=%async_computation.2 | async-start | bytes 4718592 | tf_op jit(solution)/shard_map/all_gather | solution.py:17
  7.9 80.9 %all-gather.7.cloned.1.call-start = ((), (), s32[]{:S(2)}) async-start(), calls=%async_computation.3 | async-start | bytes 2359296 | tf_op jit(solution)/shard_map/all_gather | solution.py:22
  8.7 132.8 %all-reduce.7.cloned.1.call-start = ((), (), s32[]{:S(2)}) async-start(), calls=%async_computation.4 | async-start | bytes 524288 | tf_op jit(solution)/shard_map/psum | solution.py:29
  98.9 100.1 %all-reduce.9.cloned.1.call-start = ((), (), s32[]{:S(2)}) async-start(), calls=%async_computation.5 | async-start | bytes 131072 | tf_op jit(solution)/shard_map/psum | solution.py:33
  143.7 133.6 %reduce-scatter.3.cloned.1.call-start = ((), (), s32[]{:S(2)}) async-start(), calls=%async_computation.6 | async-start | bytes 2359296 | tf_op jit(solution)/shard_map/reduce_scatter | solution.py:43
  242.1 79.7 %all-reduce.11.cloned.1.call-start = ((), (), s32[]{:S(2)}) async-start(), calls=%async_computation.7 | async-start | bytes 524288 | tf_op jit(solution)/shard_map/psum | solution.py:44
  277.3 75.7 %all-gather.9.cloned.1.call-start = ((), (), s32[]{:S(2)}) async-start(), calls=%async_computation.8 | async-start | bytes 2359296 | tf_op jit(solution)/shard_map/all_gather | solution.py:45
  323.4 82.3 %all-reduce.13.cloned.1.call-start = ((), (), s32[]{:S(2)}) async-start(), calls=%async_computation.9 | async-start | bytes 524288 | tf_op jit(solution)/shard_map/psum | solution.py:29
  363.2 100.2 %all-reduce.15.cloned.1.call-start = ((), (), s32[]{:S(2)}) async-start(), calls=%async_computation.10 | async-start | bytes 131072 | tf_op jit(solution)/shard_map/psum | solution.py:33
  408.0 133.4 %reduce-scatter.5.cloned.1.call-start = ((), (), s32[]{:S(2)}) async-start(), calls=%async_computation.11 | async-start | bytes 2359296 | tf_op jit(solution)/shard_map/reduce_scatter | solution.py:43
  506.2 79.9 %all-reduce.17.cloned.1.call-start = ((), (), s32[]{:S(2)}) async-start(), calls=%async_computation.12 | async-start | bytes 524288 | tf_op jit(solution)/shard_map/psum | solution.py:44
  541.5 75.8 %all-gather.11.cloned.1.call-start = ((), (), s32[]{:S(2)}) async-start(), calls=%async_computation.13 | async-start | bytes 2359296 | tf_op jit(solution)/shard_map/all_gather | solution.py:45
Sparse Core Ops, SparseCore 0:
  9.6 49.5 all-gather.4
  60.8 27.9 all-gather.6
  99.0 42.4 all-reduce.6
  144.2 54.6 all-reduce.8
  242.2 35.0 reduce-scatter.2
  280.1 41.5 all-reduce.10
  323.9 29.1 all-gather.8
  363.3 42.4 all-reduce.12
  408.6 54.6 all-reduce.14
  506.3 35.1 reduce-scatter.4
  544.4 41.6 all-reduce.16
  588.1 29.1 all-gather.10
where the time goes:
time: 644 us; the launch traced here: 639 us
  waiting for transfers between devices  485 us (75%)
  matrix products  86.1 us (13%)
  other arithmetic  50.8 us (8%)
  between operations  14.5 us (2%)
    psum x2, waiting for transfers between devices, per_device(): gram_matrix = lax.psum(gram_local, 'rows')  110 us
    psum x2, waiting for transfers between devices, per_device(): own_rows = lax.psum(own_rows, 'dp') / replicas  88.9 us
    psum x2, waiting for transfers between devices, per_device(): left_factor = lax.psum(local_term, 'dp') / replicas  85.1 us
    reduce_scatter x2, waiting for transfers between devices, per_device(): lax.psum_scatter(right_term, 'rows', scatter_dimension=0, tiled=True)  70.4 us
    all_gather x2, waiting for transfers between devices, per_device(): right_full = lax.all_gather(own_rows, 'rows', axis=0, tiled=True)  59.1 us
    all_gather x1, waiting for transfers between devices, per_device(): lax.all_gather(activations, 'rows', axis=1, tiled=True)  50.5 us
    dot_general x2, matrix products, per_device(): lax.dot_general(merged, left_factor, (((0,), (0,)), ((), ())), precision=...  33.8 us
    another operation x6, other arithmetic, per_device(): cholesky_lower = jnp.linalg.cholesky(gram_matrix)  24.8 us
  transfers between devices with their start and end apart: 12, of which 12 were waited for; matrix products, arithmetic and copies ran while one was open for 2% of the time, Pallas kernels for 0%

commit v1 on v0

v1 whole, which is shorter than its diff:
```python
import jax
import jax.numpy as jnp
from jax import lax
from jax.sharding import PartitionSpec as P

PASSES = 2
MOMENTUM_RATE = 0.9
HIGHEST = lax.Precision.HIGHEST
F32 = jnp.float32


def ring_masks(size):
    masks, mask = [], 1
    while mask < size:
        masks.append(mask)
        mask = 2 * mask + 1
    return masks


def swap(value, axis, mask):
    size = lax.axis_size(axis)
    return lax.ppermute(value, axis, [(i, i ^ mask) for i in range(size)])


def parts_of(array, count, dim=0):
    return jnp.split(array, count, axis=dim) if count > 1 else [array]


def rotations(masks):
    count = 1 << (len(masks).bit_length() - 1)
    return [masks[i:] + masks[:i] for i in range(count)]


def all_reduce(array, axis, masks):
    if not masks:
        return array
    orders = rotations(masks)
    parts = parts_of(array, len(orders))
    for step in range(len(masks)):
        came = [swap(part, axis, order[step]) for part, order in zip(parts, orders)]
        parts = [part + other for part, other in zip(parts, came)]
    return jnp.concatenate(parts, axis=0) if len(parts) > 1 else parts[0]


def all_gather(array, axis, masks):
    if not masks:
        return {0: array}
    orders = rotations(masks)
    held = [{0: part} for part in parts_of(array, len(orders))]
    for step in range(len(masks)):
        fresh = []
        for blocks, order in zip(held, orders):
            keys = sorted(blocks)
            came = swap(jnp.stack([blocks[k] for k in keys]), axis, order[step])
            fresh.append({k ^ order[step]: came[n] for n, k in enumerate(keys)})
        for blocks, extra in zip(held, fresh):
            blocks.update(extra)
    return {k: jnp.concatenate([blocks[k] for blocks in held], axis=0) for k in held[0]}


def span_of(masks):
    keys = [0]
    for mask in masks:
        keys = keys + [k ^ mask for k in keys]
    return sorted(keys)


def to_half(array):
    top = jnp.max(jnp.abs(array))
    power = jnp.where(top > 0, 13.0 - jnp.floor(jnp.log2(jnp.maximum(top, 1e-37))), 0.0)
    power = jnp.clip(power, -100.0, 100.0)
    body = (array * jnp.exp2(power)).astype(jnp.float16)
    tail = jnp.full((16, array.shape[-1]), power, jnp.float16)
    return jnp.concatenate([body, tail], axis=0)


def from_half(message):
    power = message[-1, 0].astype(F32)
    return message[:-16].astype(F32) * jnp.exp2(-power)


def reduce_scatter_half(pieces, axis, masks):
    orders = rotations(masks)
    done = []
    split = {k: parts_of(piece, len(orders)) for k, piece in pieces.items()}
    held = [{k: split[k][n] for k in split} for n in range(len(orders))]
    coords = []
    for order in orders:
        table = {0: ()}
        for mask in order:
            table = {**{k: v + (0,) for k, v in table.items()}, **{k ^ mask: v + (1,) for k, v in table.items()}}
        coords.append(table)
    for step in range(len(masks)):
        arrivals = []
        for blocks, order, table in zip(held, orders, coords):
            away = sorted(k for k in blocks if table[k][step])
            message = jnp.concatenate([blocks[k] for k in away], axis=0)
            arrivals.append((away, swap(to_half(message), axis, order[step])))
        fresh = []
        for blocks, order, (away, message) in zip(held, orders, arrivals):
            came = parts_of(from_half(message), len(away))
            fresh.append({k ^ order[step]: blocks[k ^ order[step]] + came[n] for n, k in enumerate(away)})
        held = fresh
    return jnp.concatenate([blocks[0] for blocks in held], axis=0)


def from_relative(blocks, index, count):
    table = jnp.stack([blocks[k] for k in range(count)])
    order = jnp.bitwise_xor(jnp.arange(count), index)
    return jnp.take(table, order, axis=0)


def dot(a, b, dims, precision=HIGHEST):
    return lax.dot_general(a, b, (dims, ((), ())), precision=precision, preferred_element_type=F32)


def per_device(dp_masks, chip_masks, grad_out, activations, error_feedback, momentum, right_factor):
    replicas, row_blocks = lax.axis_size("dp"), lax.axis_size("rows")
    me_dp, me_row = lax.axis_index("dp"), lax.axis_index("rows")
    error = error_feedback[0]
    inputs = error.shape[1]
    width = inputs // replicas

    tokens = activations.shape[0]
    row_masks = chip_masks + [1]
    gathered = all_gather(activations, "rows", chip_masks)
    gathered.update({k ^ 1: swap(block, "rows", 1) for k, block in list(gathered.items())})
    full_act = from_relative(gathered, me_row, row_blocks)
    full_act = jnp.moveaxis(full_act, 0, 1).reshape(tokens, inputs)
    right_all = all_gather(right_factor, "rows", chip_masks)
    right_all.update({k ^ 1: swap(block, "rows", 1) for k, block in list(right_all.items())})
    right_all = from_relative(right_all, me_row, row_blocks).reshape(inputs, -1)
    right = lax.dynamic_slice_in_dim(right_all, me_dp * width, width, 0)

    merged = lax.dot_general(grad_out, full_act, (((0,), (0,)), ((), ())), preferred_element_type=F32) + error
    pieces = {
        k: lax.dynamic_slice_in_dim(merged, jnp.bitwise_xor(me_dp, k) * width, width, 1)
        for k in span_of(dp_masks)
    }
    mean = reduce_scatter_half(pieces, "dp", dp_masks) / replicas

    own_half = me_row % 2
    for _ in range(PASSES):
        left = all_reduce(dot(mean, right, ((1,), (0,))), "dp", dp_masks)
        term = dot(mean, left, ((0,), (0,)))
        gram = dot(left, left, ((0,), (0,)))
        both = jnp.concatenate([term, gram], axis=0)
        half = both.shape[0] // 2
        keep = lax.dynamic_slice_in_dim(both, own_half * half, half, 0)
        give = lax.dynamic_slice_in_dim(both, (1 - own_half) * half, half, 0)
        keep = all_reduce(keep + swap(give, "rows", 1), "rows", chip_masks)
        other = swap(keep, "rows", 1)
        both = jnp.where(own_half == 0, jnp.concatenate([keep, other]), jnp.concatenate([other, keep]))
        term, gram = both[:width], both[width:]
        lower = jnp.linalg.cholesky(gram)
        right = jax.scipy.linalg.solve_triangular(lower, term.T, lower=True).T
    left = jax.scipy.linalg.solve_triangular(lower, left.T, lower=True).T
    full_right = from_relative(all_gather(right, "dp", dp_masks), me_dp, replicas).reshape(inputs, -1)
    own_rows = lax.dynamic_slice_in_dim(full_right, me_row * right_factor.shape[0], right_factor.shape[0], 0)
    approx = dot(left, full_right, ((1,), (1,)))
    new_error = (merged - approx)[None]
    new_momentum = (MOMENTUM_RATE * momentum.astype(F32) + approx).astype(jnp.bfloat16)
    return (new_error, new_momentum, own_rows)


def solution(mesh):
    replicas, row_blocks = mesh.shape["dp"], mesh.shape["rows"]
    side = 1 << ((replicas.bit_length() - 1) // 2)
    dp_masks = ring_masks(side) + [m * side for m in ring_masks(replicas // side)]
    chip_masks = [2 * m for m in ring_masks(row_blocks // 2)]

    def body(*args):
        return per_device(dp_masks, chip_masks, *args)

    return jax.shard_map(
        body,
        mesh=mesh,
        in_specs=(
            P("dp", "rows"),
            P("dp", "rows"),
            P("dp", "rows", None),
            P("rows", None),
            P("rows", None),
        ),
        out_specs=(P("dp", "rows", None), P("rows", None), P("rows", None)),
        check_vma=False,
    )
```

time: 644 us -> 356 us (0.55)
  waiting for transfers between devices: 485 us -> 137 us
  matrix products: 86.1 us -> 30.8 us
  local copies, waits for them, and re-layouts: 1.86 us -> 49.6 us
  starting transfers between devices: 0.95 us -> 44.7 us
  other arithmetic: 50.8 us -> 80.9 us
    psum x6 -> x0, waiting for transfers between devices: 284 us -> none  [the longest x2 110 us: per_device(): gram_matrix = lax.psum(gram_local, 'rows')]
    ppermute x0 -> x44, waiting for transfers between devices: none -> 137 us  [swap(): return lax.ppermute(value, axis, [(i, i ^ mask) for i in range(size)])]
    all_gather x4 -> x0, waiting for transfers between devices: 129 us -> none  [the longest x2 59.1 us: per_device(): right_full = lax.all_gather(own_rows, 'rows', axis=0, tiled=True)]
    reduce_scatter x2 -> x0, waiting for transfers between devices: 70.4 us -> none  [per_device(): lax.psum_scatter(right_term, 'rows', scatter_dimension=0, tiled=True)]
    dot_general x8, matrix products: 83.3 us -> 29.1 us  [the longest x7 22 us: dot(): lax.dot_general(a, b, (dims, ((), ())), precision=precision, preferred_el...]
    ppermute x0 -> x44, starting transfers between devices: none -> 44.7 us  [swap(): return lax.ppermute(value, axis, [(i, i ^ mask) for i in range(size)])]
    unnamed x2 -> x30, local copies, waits for them, and re-layouts: 0.01 us -> 14.4 us
    gather x0 -> x4, local copies, waits for them, and re-layouts: none -> 12.5 us  [from_relative(): return jnp.take(table, order, axis=0)]
  transfers between devices with their start and end apart: 12 -> 44, of which waited for: 12 -> 32; matrix products, arithmetic and copies ran while one was open for 2% -> 20% of each run, Pallas kernels for 0% -> 0%
where the time goes in v1:
time: 356 us; the launch traced here: 352 us
  waiting for transfers between devices  137 us (38%)
  other arithmetic  80.9 us (23%)
  local copies, waits for them, and re-layouts  49.6 us (14%)
  starting transfers between devices  44.7 us (13%)
  matrix products  30.8 us (9%)
  between operations  9.5 us (3%)
    ppermute x44, waiting for transfers between devices, swap(): return lax.ppermute(value, axis, [(i, i ^ mask) for i in range(size)])  137 us
    ppermute x44, starting transfers between devices, swap(): return lax.ppermute(value, axis, [(i, i ^ mask) for i in range(size)])  44.7 us
    another operation x6, other arithmetic, per_device(): lower = jnp.linalg.cholesky(gram)  24.8 us
    dot_general x7, matrix products, dot(): lax.dot_general(a, b, (dims, ((), ())), precision=precision, preferred_el...  22 us
    unnamed x30, local copies, waits for them, and re-layouts  14.4 us
    gather x4, local copies, waits for them, and re-layouts, from_relative(): return jnp.take(table, order, axis=0)  12.5 us
    another operation x2, other arithmetic, per_device(): right = jax.scipy.linalg.solve_triangular(lower, term.T, lower=True).T  10.5 us
    another operation x2, other arithmetic, per_device(): left = jax.scipy.linalg.solve_triangular(lower, left.T, lower=True).T  10.5 us
  transfers between devices with their start and end apart: 44, of which 32 were waited for; matrix products, arithmetic and copies ran while one was open for 20% of the time, Pallas kernels for 0%

profile of v1, /device:TPU:0, one launch (start us, length us, event | category | flops | bytes accessed | tf_op | source)
XLA Modules:
  0.0 352.2 jit_solution(17629655916198621547)
XLA Ops:
  2.3 4.7 %collective-permute-start.2 = (bf16[1,256,512]{2,1,0:T(8,128)(2,1)S(1)}, bf16[1,256,512]{2,1,0:T(8,128)(2,1)S(1)}, u32[]{:S(2)}, u32[]{:S(2)}) collective-permute-start(bf16[1,256,512]{2,1,0:T(8,128)(2,1)S(1)} %get-tuple-element.26), channel_id=1, source_target_pairs={{0,6},{1,7},{2,4},{3,5},{4,2},{5,3},{6,0},{7,1},{8,14},{9,15},{10,... | collective-permute-start | bytes 786440 | tf_op jit(solution)/shard_map/ppermute | solution.py:22
  7.2 1.6 slice_bitcast_fusion.21
  9.5 1.9 bitcast_dynamic-update-slice_fusion.7
  12.2 2.0 collective-permute-done.2
  14.3 5.6 %collective-permute-start.3 = (bf16[2,256,512]{2,1,0:T(8,128)(2,1)S(1)}, bf16[2,256,512]{2,1,0:T(8,128)(2,1)S(1)}, u32[]{:S(2)}, u32[]{:S(2)}) collective-permute-start(bf16[2,256,512]{2,1,0:T(8,128)(2,1)S(1)} %pad_maximum_fusion.3), channel_id=1, source_target_pairs={{0,2},{1,3},{2,0},{3,1},{4,6},{5,7},{6,4},{7,5},{8,10},{9,11},{10,... | collective-permute-start | bytes 1572872 | tf_op jit(solution)/shard_map/ppermute | solution.py:22
  20.0 1.9 collective-permute-start.13
  23.5 10.2 %collective-permute-done.3 = bf16[2,256,512]{2,1,0:T(8,128)(2,1)S(1)} collective-permute-done((bf16[2,256,512]{2,1,0:T(8,128)(2,1)S(1)}, bf16[2,256,512]{2,1,0:T(8,128)(2,1)S(1)}, u32[]{:S(2)}, u32[]{:S(2)}) %collective-permute-start.3) | collective-permute-done | bytes 524320 | tf_op jit(solution)/shard_map/ppermute | solution.py:22
  33.9 13.8 %collective-permute-done.5 = bf16[2,256,512]{2,1,0:T(8,128)(2,1)S(1)} collective-permute-done((bf16[2,256,512]{2,1,0:T(8,128)(2,1)S(1)}, bf16[2,256,512]{2,1,0:T(8,128)(2,1)S(1)}, u32[]{:S(2)}, u32[]{:S(2)}) %collective-permute-start.5) | collective-permute-done | bytes 524320 | tf_op jit(solution)/shard_map/ppermute | solution.py:22
  53.5 5.0 %gather_fusion = bf16[8,512,512]{2,1,0:T(8,128)(2,1)} fusion(bf16[8,512,512]{2,1,0:T(8,128)(2,1)} %bitcast_dynamic-update-slice_fusion, s32[1024]{0:T(1024)S(1)} %pad_clamp_fusion.1), kind=kCustom, calls=%fused_computation | custom fusion | bytes 8388640 | tf_op jit(solution)/shard_map/jit(_take)/gather | solution.py:110
  58.5 4.7 %select_bitcast_fusion = bf16[512,8,512]{2,0,1:T(8,128)(2,1)} fusion(bf16[8,512,512]{2,1,0:T(8,128)(2,1)} %gather_fusion, pred[8]{0:T(512)(128)(4,1)S(1)} %compare_and_fusion.1), kind=kLoop, calls=%fused_computation.6 | loop fusion | flops 2097152 | bytes 8388616 | tf_op jit(solution)/shard_map/jit(_take)/select_n | solution.py:110
  63.2 6.6 %copy.21 = bf16[512,8,512]{0,2,1:T(8,128)(2,1)} copy(bf16[512,8,512]{2,0,1:T(8,128)(2,1)} %select_bitcast_fusion) | data formatting | bytes 8388608 | tf_op jit(solution)/shard_map/jit(_take)/select_n | solution.py:110
  69.8 7.1 %bitcast_add_fusion = f32[512,4096]{1,0:T(8,128)S(1)} fusion(f32[1,512,4096]{2,1,0:T(8,128)} %param.10, bf16[512,4096]{0,1:T(8,128)(2,1)} %bitcast.144, bf16[512,512]{1,0:T(8,128)(2,1)S(1)} %copy-done), kind=kOutput, calls=%fused_computation.3 | convolution fusion | flops 2149580800 | bytes 21495808 | tf_op jit(solution)/shard_map/dot_general | solution.py:135
  77.5 2.8 copy-done.2
  85.8 1.8 multiply_convert_fusion
  95.8 3.6 %collective-permute-start.17 = (f32[2,256,128]{2,1,0:T(8,128)S(1)}, f32[2,256,128]{2,1,0:T(8,128)S(1)}, u32[]{:S(2)}, u32[]{:S(2)}) collective-permute-start(f32[2,256,128]{2,1,0:T(8,128)S(1)} %pad_maximum_fusion.14), channel_id=1, source_target_pairs={{0,6},{1,7},{2,4},{3,5},{4,2},{5,3},{6,0},{7,1},{8,14},{9,15},{10,... | collective-permute-start | bytes 786440 | tf_op jit(solution)/shard_map/ppermute | solution.py:22
  99.4 1.7 bitcast_dynamic-update-slice_fusion.14
  101.0 2.4 collective-permute-done.15
  104.2 6.7 %collective-permute-done.17 = f32[2,256,128]{2,1,0:T(8,128)S(1)} collective-permute-done((f32[2,256,128]{2,1,0:T(8,128)S(1)}, f32[2,256,128]{2,1,0:T(8,128)S(1)}, u32[]{:S(2)}, u32[]{:S(2)}) %collective-permute-start.17) | collective-permute-done | bytes 262176 | tf_op jit(solution)/shard_map/ppermute | solution.py:22
  111.7 3.3 collective-permute-done.10
  116.8 1.9 collective-permute-done.8
  121.7 3.7 %abs_reduce_fusion.3 = (f32[]{:T(128)}, f32[]{:T(128)}) fusion(f32[512,1024]{1,0:T(8,128)S(1)} %convert_multiply_fusion.1, f32[512,4096]{1,0:T(8,128)} %copy-done.2, s32[]{:T(128)S(6)} %select_n.121, f32[512,1024]{1,0:T(8,128)S(1)} %convert_multiply_fusion, s32[]{:T(128)S(6)} %add.200, s32[]{:T(128)S(6)} %select_n.118), kind=kLoop, calls=%fused_computation.27 | loop fusion | flops 1572862 | bytes 4194324 | tf_op jit(solution)/shard_map/reduce_max | solution.py:69
  130.2 1.7 bitcast_dynamic-update-slice_fusion.12
  133.9 7.8 %collective-permute-done.9 = f16[272,1024]{1,0:T(8,128)(2,1)S(1)} collective-permute-done((f16[272,1024]{1,0:T(8,128)(2,1)S(1)}, f16[272,1024]{1,0:T(8,128)(2,1)S(1)}, u32[]{:S(2)}, u32[]{:S(2)}) %collective-permute-start.9) | collective-permute-done | bytes 557088 | tf_op jit(solution)/shard_map/ppermute | solution.py:22
  142.9 2.7 fusion.1
  147.3 1.7 bitcast_dynamic-update-slice_fusion.10
  150.4 3.6 %gather_fusion.1 = f32[8,512,128]{2,1,0:T(8,128)} fusion(f32[8,512,128]{2,1,0:T(8,128)} %bitcast_dynamic-update-slice_fusion.8, s32[1024]{0:T(1024)S(1)} %pad_clamp_fusion.1), kind=kCustom, calls=%fused_computation.1 | custom fusion | bytes 4194336 | tf_op jit(solution)/shard_map/jit(_take)/gather | solution.py:110
  154.0 4.5 %collective-permute-done.11 = f16[272,1024]{1,0:T(8,128)(2,1)} collective-permute-done((f16[272,1024]{1,0:T(8,128)(2,1)S(1)}, f16[272,1024]{1,0:T(8,128)(2,1)}, u32[]{:S(2)}, u32[]{:S(2)}) %collective-permute-start.11) | collective-permute-done | bytes 557088 | tf_op jit(solution)/shard_map/ppermute | solution.py:22
  160.3 1.9 fusion
  162.2 2.9 fusion.5
  167.2 3.0 collective-permute-done.20
  170.3 2.7 collective-permute-done.22
  173.7 4.4 %collective-permute-done.23 = f32[256,128]{1,0:T(8,128)S(1)} collective-permute-done((f32[256,128]{1,0:T(8,128)S(1)}, f32[256,128]{1,0:T(8,128)S(1)}, u32[]{:S(2)}, u32[]{:S(2)}) %collective-permute-start.23) | collective-permute-done | bytes 131104 | tf_op jit(solution)/shard_map/ppermute | solution.py:22
  182.7 3.5 collective-permute-start.27
  186.2 6.1 %collective-permute-done.27 = f32[288,128]{0,1:T(8,128)S(1)} collective-permute-done((f32[288,128]{0,1:T(8,128)S(1)}, f32[288,128]{0,1:T(8,128)S(1)}, u32[]{:S(2)}, u32[]{:S(2)}) %collective-permute-start.27) | collective-permute-done | bytes 147488 | tf_op jit(solution)/shard_map/ppermute | solution.py:22
  192.3 3.4 collective-permute-done.25
  195.8 1.8 collective-permute-start.26
  197.7 7.9 %collective-permute-done.26 = f32[288,128]{0,1:T(8,128)S(1)} collective-permute-done((f32[288,128]{0,1:T(8,128)S(1)}, f32[288,128]{0,1:T(8,128)S(1)}, u32[]{:S(2)}, u32[]{:S(2)}) %collective-permute-start.26) | collective-permute-done | bytes 147488 | tf_op jit(solution)/shard_map/ppermute | solution.py:22
  205.6 1.8 collective-permute-done.28
  207.6 1.6 collective-permute-done.29
  212.5 11.7 %cholesky.44 = f32[128,128]{1,0:T(8,128)S(1)} custom-call(f32[128,128]{1,0:T(8,128)S(1)} %fusion.25), custom_call_target="Cholesky" | custom-call | tf_op jit(solution)/shard_map/jit(cholesky)/cholesky | solution.py:155
  225.6 9.8 %custom-call.11 = f32[1,128,128]{1,2,0:T(8,128)S(1)} custom-call(f32[1,128,128]{2,1,0:T(8,128)S(1)} %fusion.19), custom_call_target="InvertDiagBlocksLowerTriangular" | custom-call | tf_op jit(solution)/shard_map/jit(_solve_triangular)/triangular_solve | solution.py:156
  236.0 1.8 fusion.3
  237.9 2.0 collective-permute-start.30
  240.4 3.2 collective-permute-done.30
  246.2 4.1 %collective-permute-done.33 = f32[256,128]{1,0:T(8,128)S(1)} collective-permute-done((f32[256,128]{1,0:T(8,128)S(1)}, f32[256,128]{1,0:T(8,128)S(1)}, u32[]{:S(2)}, u32[]{:S(2)}) %collective-permute-start.33) | collective-permute-done | bytes 131104 | tf_op jit(solution)/shard_map/ppermute | solution.py:22
  253.3 1.6 collective-permute-done.34
  255.3 2.3 collective-permute-start.37
  257.9 7.1 %collective-permute-done.37 = f32[288,128]{0,1:T(8,128)S(1)} collective-permute-done((f32[288,128]{0,1:T(8,128)S(1)}, f32[288,128]{0,1:T(8,128)S(1)}, u32[]{:S(2)}, u32[]{:S(2)}) %collective-permute-start.37) | collective-permute-done | bytes 147488 | tf_op jit(solution)/shard_map/ppermute | solution.py:22
  265.0 3.4 collective-permute-done.35
  268.5 1.7 collective-permute-start.36
  270.2 8.0 %collective-permute-done.36 = f32[288,128]{0,1:T(8,128)S(1)} collective-permute-done((f32[288,128]{0,1:T(8,128)S(1)}, f32[288,128]{0,1:T(8,128)S(1)}, u32[]{:S(2)}, u32[]{:S(2)}) %collective-permute-start.36) | collective-permute-done | bytes 147488 | tf_op jit(solution)/shard_map/ppermute | solution.py:22
  278.2 2.3 collective-permute-done.38
  280.7 1.6 collective-permute-done.39
  283.0 11.7 %cholesky.55 = f32[128,128]{1,0:T(8,128)S(1)} custom-call(f32[128,128]{1,0:T(8,128)S(1)} %fusion.23), custom_call_target="Cholesky" | custom-call | tf_op jit(solution)/shard_map/jit(cholesky)/cholesky | solution.py:155
  296.1 9.8 %custom-call.9 = f32[1,128,128]{1,2,0:T(8,128)S(1)} custom-call(f32[1,128,128]{2,1,0:T(8,128)S(1)} %fusion.20), custom_call_target="InvertDiagBlocksLowerTriangular" | custom-call | tf_op jit(solution)/shard_map/jit(_solve_triangular)/triangular_solve | solution.py:157
  307.2 1.7 collective-permute-start.40
  309.0 6.0 %collective-permute-done.41 = f32[1,512,128]{1,2,0:T(8,128)S(1)} collective-permute-done((f32[1,512,128]{1,2,0:T(8,128)S(1)}, f32[1,512,128]{1,2,0:T(8,128)S(1)}, u32[]{:S(2)}, u32[]{:S(2)}) %collective-permute-start.41) | collective-permute-done | bytes 262176 | tf_op jit(solution)/shard_map/ppermute | solution.py:22
  315.0 1.8 collective-permute-start.42
  318.6 9.6 %collective-permute-done.42 = f32[2,512,128]{1,2,0:T(8,128)S(1)} collective-permute-done((f32[2,512,128]{1,2,0:T(8,128)S(1)}, f32[2,512,128]{1,2,0:T(8,128)S(1)}, u32[]{:S(2)}, u32[]{:S(2)}) %collective-permute-start.42) | collective-permute-done | bytes 524320 | tf_op jit(solution)/shard_map/ppermute | solution.py:22
  328.3 2.5 collective-permute-done.43
  332.2 2.0 gather_fusion.2
  334.2 1.9 copy.28
  336.1 2.1 bitcast_select_fusion
  339.0 13.0 %add_convert_fusion = (bf16[512,4096]{1,0:T(8,128)(2,1)}, f32[1,512,4096]{2,1,0:T(8,128)}) fusion(bf16[512,4096]{1,0:T(8,128)(2,1)S(1)} %copy-done.7, f32[512,4096]{1,0:T(8,128)} %copy-done.2, f32[128,512]{1,0:T(8,128)S(1)} %fusion.17, f32[4096,128]{1,0:T(8,128)S(1)} %bitcast_select_fusion), kind=kOutput, calls=%fused_computation.4 | convolution fusion | flops 3231711232 | bytes 27525120 | tf_op jit(solution)/shard_map/dot_general | solution.py:114
  (176 shorter events, 64.0 us)
Async XLA Ops:
  0.6 69.1 %copy-start = (bf16[512,512]{1,0:T(8,128)(2,1)S(1)}, bf16[512,512]{1,0:T(8,128)(2,1)}, u32[]{:S(2)}) copy-start(bf16[512,512]{1,0:T(8,128)(2,1)} %param.8) | copy-start | bytes 1572868
  0.6 10.8 %copy-start.8 = (f32[512,128]{1,0:T(8,128)S(1)}, f32[512,128]{1,0:T(8,128)}, u32[]{:S(2)}) copy-start(f32[512,128]{1,0:T(8,128)} %param.12) | copy-start | bytes 786436
  0.7 21.2 %collective-permute-start = (bf16[512,512]{1,0:T(8,128)(2,1)}, bf16[512,512]{1,0:T(8,128)(2,1)S(1)}, u32[]{:S(2)}, u32[]{:S(2)}) collective-permute-start(bf16[512,512]{1,0:T(8,128)(2,1)} %param.9), channel_id=1, source_target_pairs={{0,1},{1,0},{2,3},{3,2},{4,5},{5,4},{6,7},{7,6},{8,9},{9,8},{10,11... | collective-permute-start | bytes 1572872 | tf_op jit(solution)/shard_map/ppermute | solution.py:22
  2.3 12.0 %collective-permute-start.2 = (bf16[1,256,512]{2,1,0:T(8,128)(2,1)S(1)}, bf16[1,256,512]{2,1,0:T(8,128)(2,1)S(1)}, u32[]{:S(2)}, u32[]{:S(2)}) collective-permute-start(bf16[1,256,512]{2,1,0:T(8,128)(2,1)S(1)} %get-tuple-element.26), channel_id=1, source_target_pairs={{0,6},{1,7},{2,4},{3,5},{4,2},{5,3},{6,0},{7,1},{8,14},{9,15},{10,... | collective-permute-start | bytes 786440 | tf_op jit(solution)/shard_map/ppermute | solution.py:22
  7.0 13.0 %collective-permute-start.1 = (bf16[1,256,512]{2,1,0:T(8,128)(2,1)S(1)}, bf16[1,256,512]{2,1,0:T(8,128)(2,1)S(1)}, u32[]{:S(2)}, u32[]{:S(2)}) collective-permute-start(bf16[1,256,512]{2,1,0:T(8,128)(2,1)S(1)} %get-tuple-element.25), channel_id=1, source_target_pairs={{0,2},{1,3},{2,0},{3,1},{4,6},{5,7},{6,4},{7,5},{8,10},{9,11},{10,... | collective-permute-start | bytes 786440 | tf_op jit(solution)/shard_map/ppermute | solution.py:22
  7.0 92.4 %collective-permute-start.12 = (f32[512,128]{1,0:T(8,128)}, f32[512,128]{1,0:T(8,128)}, u32[]{:S(2)}, u32[]{:S(2)}) collective-permute-start(f32[512,128]{1,0:T(8,128)} %param.12), channel_id=1, source_target_pairs={{0,1},{1,0},{2,3},{3,2},{4,5},{5,4},{6,7},{7,6},{8,9},{9,8},{10,11... | collective-permute-start | bytes 786440 | tf_op jit(solution)/shard_map/ppermute | solution.py:22
  8.8 86.0 %collective-permute-start.14 = (f32[1,256,128]{2,1,0:T(8,128)}, f32[1,256,128]{2,1,0:T(8,128)S(1)}, u32[]{:S(2)}, u32[]{:S(2)}) collective-permute-start(f32[1,256,128]{2,1,0:T(8,128)} %get-tuple-element.48), channel_id=1, source_target_pairs={{0,6},{1,7},{2,4},{3,5},{4,2},{5,3},{6,0},{7,1},{8,14},{9,15},{10,... | collective-permute-start | bytes 393224 | tf_op jit(solution)/shard_map/ppermute | solution.py:22
  14.3 19.5 %collective-permute-start.3 = (bf16[2,256,512]{2,1,0:T(8,128)(2,1)S(1)}, bf16[2,256,512]{2,1,0:T(8,128)(2,1)S(1)}, u32[]{:S(2)}, u32[]{:S(2)}) collective-permute-start(bf16[2,256,512]{2,1,0:T(8,128)(2,1)S(1)} %pad_maximum_fusion.3), channel_id=1, source_target_pairs={{0,2},{1,3},{2,0},{3,1},{4,6},{5,7},{6,4},{7,5},{8,10},{9,11},{10,... | collective-permute-start | bytes 1572872 | tf_op jit(solution)/shard_map/ppermute | solution.py:22
  20.0 75.8 %collective-permute-start.13 = (f32[1,256,128]{2,1,0:T(8,128)S(1)}, f32[1,256,128]{2,1,0:T(8,128)S(1)}, u32[]{:S(2)}, u32[]{:S(2)}) collective-permute-start(f32[1,256,128]{2,1,0:T(8,128)S(1)} %get-tuple-element.47), channel_id=1, source_target_pairs={{0,2},{1,3},{2,0},{3,1},{4,6},{5,7},{6,4},{7,5},{8,10},{9,11},{10,... | collective-permute-start | bytes 393224 | tf_op jit(solution)/shard_map/ppermute | solution.py:22
  21.9 25.8 %collective-permute-start.5 = (bf16[2,256,512]{2,1,0:T(8,128)(2,1)S(1)}, bf16[2,256,512]{2,1,0:T(8,128)(2,1)S(1)}, u32[]{:S(2)}, u32[]{:S(2)}) collective-permute-start(bf16[2,256,512]{2,1,0:T(8,128)(2,1)S(1)} %pad_maximum_fusion.5), channel_id=1, source_target_pairs={{0,6},{1,7},{2,4},{3,5},{4,2},{5,3},{6,0},{7,1},{8,14},{9,15},{10,... | collective-permute-start | bytes 1572872 | tf_op jit(solution)/shard_map/ppermute | solution.py:22
  33.8 14.9 %collective-permute-start.4 = (bf16[512,512]{1,0:T(8,128)(2,1)S(1)}, bf16[512,512]{1,0:T(8,128)(2,1)S(1)}, u32[]{:S(2)}, u32[]{:S(2)}) collective-permute-start(bf16[512,512]{1,0:T(8,128)(2,1)S(1)} %pad_maximum_fusion.4), channel_id=1, source_target_pairs={{0,1},{1,0},{2,3},{3,2},{4,5},{5,4},{6,7},{7,6},{8,9},{9,8},{10,11... | collective-permute-start | bytes 1572872 | tf_op jit(solution)/shard_map/ppermute | solution.py:22
  47.8 3.2 collective-permute-start.6
  48.8 3.9 %collective-permute-start.7 = (bf16[512,512]{1,0:T(8,128)(2,1)S(1)}, bf16[512,512]{1,0:T(8,128)(2,1)S(1)}, u32[]{:S(2)}, u32[]{:S(2)}) collective-permute-start(bf16[512,512]{1,0:T(8,128)(2,1)S(1)} %pad_maximum_fusion.7), channel_id=1, source_target_pairs={{0,1},{1,0},{2,3},{3,2},{4,5},{5,4},{6,7},{7,6},{8,9},{9,8},{10,11... | collective-permute-start | bytes 1572872 | tf_op jit(solution)/shard_map/ppermute | solution.py:22
  76.8 3.4 copy-start.2
  80.2 1.0 copy-start.5
  80.2 1.3 copy-start.6
  88.8 26.1 %collective-permute-start.10 = (f16[528,1024]{1,0:T(8,128)(2,1)}, f16[528,1024]{1,0:T(8,128)(2,1)}, u32[]{:S(2)}, u32[]{:S(2)}) collective-permute-start(f16[528,1024]{1,0:T(8,128)(2,1)} %concatenate.92), channel_id=1, source_target_pairs={{0,16},{8,24},{16,0},{24,8},{1,17},{9,25},{17,1},{25,9},{2,18},{10... | collective-permute-start | bytes 3244040 | tf_op jit(solution)/shard_map/ppermute | solution.py:22
  93.2 25.6 %collective-permute-start.8 = (f16[528,1024]{1,0:T(8,128)(2,1)S(1)}, f16[528,1024]{1,0:T(8,128)(2,1)S(1)}, u32[]{:S(2)}, u32[]{:S(2)}) collective-permute-start(f16[528,1024]{1,0:T(8,128)(2,1)S(1)} %concatenate.89), channel_id=1, source_target_pairs={{0,8},{8,0},{16,24},{24,16},{1,9},{9,1},{17,25},{25,17},{2,10},{10... | collective-permute-start | bytes 3244040 | tf_op jit(solution)/shard_map/ppermute | solution.py:22
  95.7 7.7 %collective-permute-start.15 = (f32[2,256,128]{2,1,0:T(8,128)S(1)}, f32[2,256,128]{2,1,0:T(8,128)S(1)}, u32[]{:S(2)}, u32[]{:S(2)}) collective-permute-start(f32[2,256,128]{2,1,0:T(8,128)S(1)} %pad_maximum_fusion.12), channel_id=1, source_target_pairs={{0,2},{1,3},{2,0},{3,1},{4,6},{5,7},{6,4},{7,5},{8,10},{9,11},{10,... | collective-permute-start | bytes 786440 | tf_op jit(solution)/shard_map/ppermute | solution.py:22
  95.8 15.1 %collective-permute-start.17 = (f32[2,256,128]{2,1,0:T(8,128)S(1)}, f32[2,256,128]{2,1,0:T(8,128)S(1)}, u32[]{:S(2)}, u32[]{:S(2)}) collective-permute-start(f32[2,256,128]{2,1,0:T(8,128)S(1)} %pad_maximum_fusion.14), channel_id=1, source_target_pairs={{0,6},{1,7},{2,4},{3,5},{4,2},{5,3},{6,0},{7,1},{8,14},{9,15},{10,... | collective-permute-start | bytes 786440 | tf_op jit(solution)/shard_map/ppermute | solution.py:22
  104.2 26.1 %collective-permute-start.16 = (f32[512,128]{1,0:T(8,128)}, f32[512,128]{1,0:T(8,128)}, u32[]{:S(2)}, u32[]{:S(2)}) collective-permute-start(f32[512,128]{1,0:T(8,128)} %pad_maximum_fusion.13), channel_id=1, source_target_pairs={{0,1},{1,0},{2,3},{3,2},{4,5},{5,4},{6,7},{7,6},{8,9},{9,8},{10,11... | collective-permute-start | bytes 786440 | tf_op jit(solution)/shard_map/ppermute | solution.py:22
  111.6 35.6 %collective-permute-start.18 = (f32[512,128]{1,0:T(8,128)}, f32[512,128]{1,0:T(8,128)}, u32[]{:S(2)}, u32[]{:S(2)}) collective-permute-start(f32[512,128]{1,0:T(8,128)} %pad_maximum_fusion.15), channel_id=1, source_target_pairs={{0,1},{1,0},{2,3},{3,2},{4,5},{5,4},{6,7},{7,6},{8,9},{9,8},{10,11... | collective-permute-start | bytes 786440 | tf_op jit(solution)/shard_map/ppermute | solution.py:22
  121.4 3.9 %copy-start.3 = (f32[512,1024]{1,0:T(8,128)}, f32[512,1024]{1,0:T(8,128)S(1)}, u32[]{:S(2)}) copy-start(f32[512,1024]{1,0:T(8,128)S(1)} %convert_multiply_fusion) | copy-start | bytes 6291460
  121.6 5.0 %copy-start.4 = (f32[512,1024]{1,0:T(8,128)}, f32[512,1024]{1,0:T(8,128)S(1)}, u32[]{:S(2)}) copy-start(f32[512,1024]{1,0:T(8,128)S(1)} %convert_multiply_fusion.1) | copy-start | bytes 6291460
  128.2 13.5 %collective-permute-start.9 = (f16[272,1024]{1,0:T(8,128)(2,1)S(1)}, f16[272,1024]{1,0:T(8,128)(2,1)S(1)}, u32[]{:S(2)}, u32[]{:S(2)}) collective-permute-start(f16[272,1024]{1,0:T(8,128)(2,1)S(1)} %concatenate.90), channel_id=1, source_target_pairs={{0,16},{8,24},{16,0},{24,8},{1,17},{9,25},{17,1},{25,9},{2,18},{10... | collective-permute-start | bytes 1671176 | tf_op jit(solution)/shard_map/ppermute | solution.py:22
  129.5 20.2 %collective-permute-start.19 = (f32[512,128]{1,0:T(8,128)}, f32[512,128]{1,0:T(8,128)S(1)}, u32[]{:S(2)}, u32[]{:S(2)}) collective-permute-start(f32[512,128]{1,0:T(8,128)} %pad_maximum_fusion.16), channel_id=1, source_target_pairs={{0,1},{1,0},{2,3},{3,2},{4,5},{5,4},{6,7},{7,6},{8,9},{9,8},{10,11... | collective-permute-start | bytes 786440 | tf_op jit(solution)/shard_map/ppermute | solution.py:22
  145.7 12.7 %collective-permute-start.11 = (f16[272,1024]{1,0:T(8,128)(2,1)S(1)}, f16[272,1024]{1,0:T(8,128)(2,1)}, u32[]{:S(2)}, u32[]{:S(2)}) collective-permute-start(f16[272,1024]{1,0:T(8,128)(2,1)S(1)} %concatenate.93), channel_id=1, source_target_pairs={{0,8},{8,0},{16,24},{24,16},{1,9},{9,1},{17,25},{25,17},{2,10},{10... | collective-permute-start | bytes 1671176 | tf_op jit(solution)/shard_map/ppermute | solution.py:22
  165.2 5.1 %collective-permute-start.20 = (f32[256,128]{1,0:T(8,128)S(1)}, f32[256,128]{1,0:T(8,128)S(1)}, u32[]{:S(2)}, u32[]{:S(2)}) collective-permute-start(f32[256,128]{1,0:T(8,128)S(1)} %get-tuple-element.41), channel_id=1, source_target_pairs={{0,8},{8,0},{16,24},{24,16},{1,9},{9,1},{17,25},{25,17},{2,10},{10... | collective-permute-start | bytes 393224 | tf_op jit(solution)/shard_map/ppermute | solution.py:22
  166.7 6.3 %collective-permute-start.22 = (f32[256,128]{1,0:T(8,128)S(1)}, f32[256,128]{1,0:T(8,128)S(1)}, u32[]{:S(2)}, u32[]{:S(2)}) collective-permute-start(f32[256,128]{1,0:T(8,128)S(1)} %get-tuple-element.42), channel_id=1, source_target_pairs={{0,16},{8,24},{16,0},{24,8},{1,17},{9,25},{17,1},{25,9},{2,18},{10... | collective-permute-start | bytes 393224 | tf_op jit(solution)/shard_map/ppermute | solution.py:22
  173.1 5.0 %collective-permute-start.23 = (f32[256,128]{1,0:T(8,128)S(1)}, f32[256,128]{1,0:T(8,128)S(1)}, u32[]{:S(2)}, u32[]{:S(2)}) collective-permute-start(f32[256,128]{1,0:T(8,128)S(1)} %get-tuple-element.40), channel_id=1, source_target_pairs={{0,8},{8,0},{16,24},{24,16},{1,9},{9,1},{17,25},{25,17},{2,10},{10... | collective-permute-start | bytes 393224 | tf_op jit(solution)/shard_map/ppermute | solution.py:22
  173.1 5.0 %collective-permute-start.21 = (f32[256,128]{1,0:T(8,128)S(1)}, f32[256,128]{1,0:T(8,128)S(1)}, u32[]{:S(2)}, u32[]{:S(2)}) collective-permute-start(f32[256,128]{1,0:T(8,128)S(1)} %get-tuple-element.39), channel_id=1, source_target_pairs={{0,16},{8,24},{16,0},{24,8},{1,17},{9,25},{17,1},{25,9},{2,18},{10... | collective-permute-start | bytes 393224 | tf_op jit(solution)/shard_map/ppermute | solution.py:22
  180.7 1.7 collective-permute-start.24
  182.7 9.6 %collective-permute-start.27 = (f32[288,128]{0,1:T(8,128)S(1)}, f32[288,128]{0,1:T(8,128)S(1)}, u32[]{:S(2)}, u32[]{:S(2)}) collective-permute-start(f32[288,128]{0,1:T(8,128)S(1)} %get-tuple-element.33), channel_id=1, source_target_pairs={{0,6},{1,7},{2,4},{3,5},{4,2},{5,3},{6,0},{7,1},{8,14},{9,15},{10,... | collective-permute-start | bytes 442376 | tf_op jit(solution)/shard_map/ppermute | solution.py:22
  186.2 9.5 %collective-permute-start.25 = (f32[288,128]{0,1:T(8,128)S(1)}, f32[288,128]{0,1:T(8,128)S(1)}, u32[]{:S(2)}, u32[]{:S(2)}) collective-permute-start(f32[288,128]{0,1:T(8,128)S(1)} %get-tuple-element.34), channel_id=1, source_target_pairs={{0,2},{1,3},{2,0},{3,1},{4,6},{5,7},{6,4},{7,5},{8,10},{9,11},{10,... | collective-permute-start | bytes 442376 | tf_op jit(solution)/shard_map/ppermute | solution.py:22
  195.8 9.7 %collective-permute-start.26 = (f32[288,128]{0,1:T(8,128)S(1)}, f32[288,128]{0,1:T(8,128)S(1)}, u32[]{:S(2)}, u32[]{:S(2)}) collective-permute-start(f32[288,128]{0,1:T(8,128)S(1)} %get-tuple-element.32), channel_id=1, source_target_pairs={{0,6},{1,7},{2,4},{3,5},{4,2},{5,3},{6,0},{7,1},{8,14},{9,15},{10,... | collective-permute-start | bytes 442376 | tf_op jit(solution)/shard_map/ppermute | solution.py:22
  197.7 9.7 %collective-permute-start.28 = (f32[288,128]{0,1:T(8,128)S(1)}, f32[288,128]{0,1:T(8,128)S(1)}, u32[]{:S(2)}, u32[]{:S(2)}) collective-permute-start(f32[288,128]{0,1:T(8,128)S(1)} %get-tuple-element.31), channel_id=1, source_target_pairs={{0,2},{1,3},{2,0},{3,1},{4,6},{5,7},{6,4},{7,5},{8,10},{9,11},{10,... | collective-permute-start | bytes 442376 | tf_op jit(solution)/shard_map/ppermute | solution.py:22
  207.5 1.7 collective-permute-start.29
  237.9 5.8 %collective-permute-start.30 = (f32[256,128]{1,0:T(8,128)S(1)}, f32[256,128]{1,0:T(8,128)S(1)}, u32[]{:S(2)}, u32[]{:S(2)}) collective-permute-start(f32[256,128]{1,0:T(8,128)S(1)} %get-tuple-element.37), channel_id=1, source_target_pairs={{0,8},{8,0},{16,24},{24,16},{1,9},{9,1},{17,25},{25,17},{2,10},{10... | collective-permute-start | bytes 393224 | tf_op jit(solution)/shard_map/ppermute | solution.py:22
  239.9 5.2 %collective-permute-start.32 = (f32[256,128]{1,0:T(8,128)S(1)}, f32[256,128]{1,0:T(8,128)S(1)}, u32[]{:S(2)}, u32[]{:S(2)}) collective-permute-start(f32[256,128]{1,0:T(8,128)S(1)} %get-tuple-element.38), channel_id=1, source_target_pairs={{0,16},{8,24},{16,0},{24,8},{1,17},{9,25},{17,1},{25,9},{2,18},{10... | collective-permute-start | bytes 393224 | tf_op jit(solution)/shard_map/ppermute | solution.py:22
  245.2 5.0 %collective-permute-start.33 = (f32[256,128]{1,0:T(8,128)S(1)}, f32[256,128]{1,0:T(8,128)S(1)}, u32[]{:S(2)}, u32[]{:S(2)}) collective-permute-start(f32[256,128]{1,0:T(8,128)S(1)} %get-tuple-element.36), channel_id=1, source_target_pairs={{0,8},{8,0},{16,24},{24,16},{1,9},{9,1},{17,25},{25,17},{2,10},{10... | collective-permute-start | bytes 393224 | tf_op jit(solution)/shard_map/ppermute | solution.py:22
  245.6 5.0 %collective-permute-start.31 = (f32[256,128]{1,0:T(8,128)S(1)}, f32[256,128]{1,0:T(8,128)S(1)}, u32[]{:S(2)}, u32[]{:S(2)}) collective-permute-start(f32[256,128]{1,0:T(8,128)S(1)} %get-tuple-element.35), channel_id=1, source_target_pairs={{0,16},{8,24},{16,0},{24,8},{1,17},{9,25},{17,1},{25,9},{2,18},{10... | collective-permute-start | bytes 393224 | tf_op jit(solution)/shard_map/ppermute | solution.py:22
  253.2 1.7 collective-permute-start.34
  255.3 9.7 %collective-permute-start.37 = (f32[288,128]{0,1:T(8,128)S(1)}, f32[288,128]{0,1:T(8,128)S(1)}, u32[]{:S(2)}, u32[]{:S(2)}) collective-permute-start(f32[288,128]{0,1:T(8,128)S(1)} %get-tuple-element.29), channel_id=1, source_target_pairs={{0,6},{1,7},{2,4},{3,5},{4,2},{5,3},{6,0},{7,1},{8,14},{9,15},{10,... | collective-permute-start | bytes 442376 | tf_op jit(solution)/shard_map/ppermute | solution.py:22
  257.5 10.9 %collective-permute-start.35 = (f32[288,128]{0,1:T(8,128)S(1)}, f32[288,128]{0,1:T(8,128)S(1)}, u32[]{:S(2)}, u32[]{:S(2)}) collective-permute-start(f32[288,128]{0,1:T(8,128)S(1)} %get-tuple-element.30), channel_id=1, source_target_pairs={{0,2},{1,3},{2,0},{3,1},{4,6},{5,7},{6,4},{7,5},{8,10},{9,11},{10,... | collective-permute-start | bytes 442376 | tf_op jit(solution)/shard_map/ppermute | solution.py:22
  268.5 9.7 %collective-permute-start.36 = (f32[288,128]{0,1:T(8,128)S(1)}, f32[288,128]{0,1:T(8,128)S(1)}, u32[]{:S(2)}, u32[]{:S(2)}) collective-permute-start(f32[288,128]{0,1:T(8,128)S(1)} %get-tuple-element.28), channel_id=1, source_target_pairs={{0,6},{1,7},{2,4},{3,5},{4,2},{5,3},{6,0},{7,1},{8,14},{9,15},{10,... | collective-permute-start | bytes 442376 | tf_op jit(solution)/shard_map/ppermute | solution.py:22
  270.2 10.3 %collective-permute-start.38 = (f32[288,128]{0,1:T(8,128)S(1)}, f32[288,128]{0,1:T(8,128)S(1)}, u32[]{:S(2)}, u32[]{:S(2)}) collective-permute-start(f32[288,128]{0,1:T(8,128)S(1)} %get-tuple-element.27), channel_id=1, source_target_pairs={{0,2},{1,3},{2,0},{3,1},{4,6},{5,7},{6,4},{7,5},{8,10},{9,11},{10,... | collective-permute-start | bytes 442376 | tf_op jit(solution)/shard_map/ppermute | solution.py:22
  280.7 1.7 collective-permute-start.39
  306.6 8.4 %collective-permute-start.41 = (f32[1,512,128]{1,2,0:T(8,128)S(1)}, f32[1,512,128]{1,2,0:T(8,128)S(1)}, u32[]{:S(2)}, u32[]{:S(2)}) collective-permute-start(f32[1,512,128]{1,2,0:T(8,128)S(1)} %get-tuple-element.20), channel_id=1, source_target_pairs={{0,16},{8,24},{16,0},{24,8},{1,17},{9,25},{17,1},{25,9},{2,18},{10... | collective-permute-start | bytes 786440 | tf_op jit(solution)/shard_map/ppermute | solution.py:22
  307.2 9.6 %collective-permute-start.40 = (f32[1,512,128]{1,2,0:T(8,128)S(1)}, f32[1,512,128]{1,2,0:T(8,128)S(1)}, u32[]{:S(2)}, u32[]{:S(2)}) collective-permute-start(f32[1,512,128]{1,2,0:T(8,128)S(1)} %get-tuple-element.19), channel_id=1, source_target_pairs={{0,8},{8,0},{16,24},{24,16},{1,9},{9,1},{17,25},{25,17},{2,10},{10... | collective-permute-start | bytes 786440 | tf_op jit(solution)/shard_map/ppermute | solution.py:22
  315.0 13.2 %collective-permute-start.42 = (f32[2,512,128]{1,2,0:T(8,128)S(1)}, f32[2,512,128]{1,2,0:T(8,128)S(1)}, u32[]{:S(2)}, u32[]{:S(2)}) collective-permute-start(f32[2,512,128]{1,2,0:T(8,128)S(1)} %pad_maximum_fusion.8), channel_id=1, source_target_pairs={{0,8},{8,0},{16,24},{24,16},{1,9},{9,1},{17,25},{25,17},{2,10},{10... | collective-permute-start | bytes 1572872 | tf_op jit(solution)/shard_map/ppermute | solution.py:22
  317.6 13.1 %collective-permute-start.43 = (f32[2,512,128]{1,2,0:T(8,128)}, f32[2,512,128]{1,2,0:T(8,128)}, u32[]{:S(2)}, u32[]{:S(2)}) collective-permute-start(f32[2,512,128]{1,2,0:T(8,128)} %pad_maximum_fusion.9), channel_id=1, source_target_pairs={{0,16},{8,24},{16,0},{24,8},{1,17},{9,25},{17,1},{25,9},{2,18},{10... | collective-permute-start | bytes 1572872 | tf_op jit(solution)/shard_map/ppermute | solution.py:22
  336.1 2.9 copy-start.7
  339.0 13.0 %copy-start.1 = (bf16[512,512]{1,0:T(8,128)(2,1)S(1)}, bf16[512,512]{1,0:T(8,128)(2,1)}, u32[]{:S(2)}) copy-start(bf16[512,512]{1,0:T(8,128)(2,1)} %param.8) | copy-start | bytes 1572868
